TPU v7x, 32 devices: a whole 2x2x4 slice. The times are simulated.
32 devices in a mesh: dp: 2 (over x), row: 4 (over z), col: 4 (over y, core).
Axes of the slice: x: 2, y: 2, z: 4, core: 2. Of those that a mesh axis runs over, the one named last changes fastest.
Arguments:
- tokens: bfloat16 [4, 2048, 2048], P('dp', 'row', 'col'), may hold values from -6 to 6
- lengths: int32 [4], P('dp'), may hold values from 682 to 2048, as said below
- cotangent: bfloat16 [4, 2048, 2048], P('dp', 'row', 'col'), may hold values from -6 to 6
- norm1_gain: float32 [2048], P('col'), may hold values from 0.25 to 1.75
- norm1_bias: float32 [2048], P('col'), may hold values from -3 to 3
- query_weight: bfloat16 [2048, 2048], P('col', 'row'), may hold values from -0.125 to 0.125
- kv_weight: bfloat16 [2048, 256], P('col'), may hold values from -0.125 to 0.125
- out_weight: bfloat16 [2048, 2048], P('row', 'col'), may hold values from -1 to 1
- norm2_gain: float32 [2048], P('col'), may hold values from 0.25 to 1.75
- norm2_bias: float32 [2048], P('col'), may hold values from -3 to 3
- up_weight: bfloat16 [2048, 8192], P('col', 'row'), may hold values from -0.125 to 0.125
- down_weight: bfloat16 [8192, 2048], P('row', 'col'), may hold values from -0.0625 to 0.0625
Outputs:
- out: bfloat16 [4, 2048, 2048], P('dp', 'row', 'col')
- grad_input: bfloat16 [4, 2048, 2048], P('dp', 'row', 'col')
- grad_norm1_gain: float32 [2048], P('col')
- grad_norm1_bias: float32 [2048], P('col')
- grad_query_weight: float32 [2048, 2048], P('col', 'row')
- grad_kv_weight: float32 [2048, 256], P('col')
- grad_out_weight: float32 [2048, 2048], P('row', 'col')
- grad_norm2_gain: float32 [2048], P('col')
- grad_norm2_bias: float32 [2048], P('col')
- grad_up_weight: float32 [2048, 8192], P('col', 'row')
- grad_down_weight: float32 [8192, 2048], P('row', 'col')
Inputs may be any that keep to these rules, and one draw needn't show every extreme that they name: `lengths`: entry s is the number of valid slots of sequence s; sequences s * 2 to s * 2 + 1 belong to index s of dp. Some sequence has all 2048 slots valid.
All inputs are finite; a program needn't handle non-finite values.
Results may differ from a plain program's by a relative error of at most 0.02.
Values may be sent and summed in bfloat16 or wider, within the bound.
A program may use at most 256 MiB of HBM per device.

v0:
```python
import jax
import jax.numpy as jnp
from jax import lax
from jax.sharding import PartitionSpec as P

eps = 1e-05
BF = jnp.bfloat16
F32 = jnp.float32


def mm(a, b, ca, cb):
    return lax.dot_general(a, b, (((ca,), (cb,)), ((), ())), preferred_element_type=F32)


def norm_stats(hidden):
    centre = jnp.mean(hidden, axis=1, keepdims=True)
    spread = jnp.mean(hidden * hidden, axis=1, keepdims=True) - centre * centre
    return (centre, lax.rsqrt(spread + eps))


def norm_apply(hidden, centre, inverse, gain, bias, keep):
    return (keep * ((hidden - centre) * inverse * gain + bias)).astype(BF)


def norm_backward(gradient, normed, inverse, gain, keep):
    masked = keep * gradient
    scaled = masked * gain
    first = jnp.mean(scaled, axis=1, keepdims=True)
    second = jnp.mean(scaled * normed, axis=1, keepdims=True)
    result = inverse * (scaled - first - normed * second)
    return (result, jnp.sum(masked * normed, axis=0), jnp.sum(masked, axis=0))


def turn(weight):
    return lax.all_to_all(weight, "col", 0, 1, tiled=True)


def turn_back(rows):
    return lax.all_to_all(rows, "col", 1, 0, tiled=True)


def gather(x, axes, dim=0):
    return lax.all_gather(x, axes, axis=dim, tiled=True)


def scatter(x, axes):
    return lax.psum_scatter(x, axes, scatter_dimension=0, tiled=True)


def pairs_allowed(first, count, keys, length):
    q = first + jnp.arange(count, dtype=jnp.int32)[:, None]
    k = jnp.arange(keys, dtype=jnp.int32)[None, :]
    return (k <= q) & (k < length)


def attend(queries, kv, lengths, first):
    b, t, width = queries.shape
    hd = kv.shape[2] // 2
    outs, logs = ([], [])
    for s in range(b):
        keys, values = (kv[s, :, :hd], kv[s, :, hd:])
        allowed = pairs_allowed(first, t, kv.shape[1], lengths[s])
        for h in range(width // hd):
            q = queries[s, :, h * hd : (h + 1) * hd]
            scores = jnp.where(allowed, mm(q, keys, 1, 1) * hd ** (-0.5), -jnp.inf)
            top = jnp.max(scores, axis=1, keepdims=True)
            log_total = top + jnp.log(jnp.sum(jnp.exp(scores - top), axis=1, keepdims=True))
            weights = jnp.exp(scores - log_total).astype(BF)
            outs.append(mm(weights, values, 1, 0).astype(BF))
            logs.append(log_total)
    n = width // hd
    out = jnp.stack([jnp.concatenate(outs[s * n : (s + 1) * n], axis=1) for s in range(b)])
    log = jnp.stack([jnp.concatenate(logs[s * n : (s + 1) * n], axis=1) for s in range(b)])
    return (out, log)


def attend_back(queries, kv, lengths, first, logs, grad):
    b, t, width = queries.shape
    hd = kv.shape[2] // 2
    scale = hd ** (-0.5)
    dqs, dkvs = ([], [])
    for s in range(b):
        keys, values = (kv[s, :, :hd], kv[s, :, hd:])
        allowed = pairs_allowed(first, t, kv.shape[1], lengths[s])
        dk = dv = 0.0
        dq = []
        for h in range(width // hd):
            q = queries[s, :, h * hd : (h + 1) * hd]
            g = grad[s, :, h * hd : (h + 1) * hd]
            scores = jnp.where(allowed, mm(q, keys, 1, 1) * scale, -jnp.inf)
            p = jnp.exp(scores - logs[s, :, h : h + 1])
            dp = mm(g, values, 1, 1)
            ds = (p * (dp - jnp.sum(p * dp, axis=1, keepdims=True))).astype(BF)
            dq.append((mm(ds, keys, 1, 0) * scale).astype(BF))
            dk = dk + mm(ds, q, 0, 0) * scale
            dv = dv + mm(p.astype(BF), g, 0, 0)
        dqs.append(jnp.concatenate(dq, axis=1))
        dkvs.append(jnp.concatenate([dk, dv], axis=1).astype(BF))
    return (jnp.stack(dqs), jnp.stack(dkvs))


def local(
    tokens,
    lengths,
    cotangent,
    norm1_gain,
    norm1_bias,
    query_weight,
    kv_weight,
    out_weight,
    norm2_gain,
    norm2_bias,
    up_weight,
    down_weight,
):
    b, t, f = tokens.shape
    nd, nr, nc = (lax.axis_size(a) for a in ("dp", "row", "col"))
    dp, row, col = (lax.axis_index(a) for a in ("dp", "row", "col"))
    m, d = (b * t, f * nc)
    own = m // nc
    hd = kv_weight.shape[1] // 2
    plane = ("dp", "col")
    slot = row * t + jnp.arange(t, dtype=jnp.int32)
    keep = (slot[None, :] < lengths[:, None]).astype(F32).reshape(m, 1)

    def mine(x):
        return lax.dynamic_slice_in_dim(x, col * own, own, 0)

    def half(w):
        n = w.shape[0] // nd
        return lax.dynamic_slice_in_dim(w, dp * n, n, 0)

    wq = gather(turn(query_weight.T), "row")
    wo = gather(turn(out_weight), "row")
    wu = gather(turn(half(up_weight.T)), "row")
    wd = gather(turn(half(down_weight)), "row")
    wkv = gather(kv_weight, "col")
    vectors = gather(jnp.stack([norm1_gain, norm1_bias, norm2_gain, norm2_bias]), "col", 1)
    gain1, bias1, gain2, bias2 = (vectors[i : i + 1] for i in range(4))
    x = gather(tokens.reshape(m, f), "col", 1)
    grad_final = (keep * cotangent.reshape(m, f).astype(F32)).astype(BF)
    grad_own = turn(grad_final)
    grad_all = gather(grad_own, plane)
    keep_own = mine(keep)
    centre, inverse = norm_stats(x.astype(F32))
    one = norm_apply(x.astype(F32), centre, inverse, gain1, bias1, keep)
    one_own = mine(one)
    queries = mm(one, wq, 1, 1).astype(BF).reshape(b, t, -1)
    kv_own = mm(one_own, wkv, 1, 0).astype(BF)
    kv = gather(kv_own, ("row", "col")).reshape(nr, b, t, 2 * hd)
    kv = kv.transpose(1, 0, 2, 3).reshape(b, nr * t, 2 * hd)
    attended, logs = attend(queries, kv, lengths, row * t)
    attended = attended.reshape(m, -1)
    x_own = mine(x).astype(F32)
    middle = x_own + scatter(mm(attended, wo, 1, 0).astype(BF), "col").astype(F32)
    centre2, inverse2 = norm_stats(middle)
    two_own = norm_apply(middle, centre2, inverse2, gain2, bias2, keep_own)
    two = gather(two_own, plane)
    sums = mm(two, wu, 1, 1)
    activated, pull = jax.vjp(lambda v: jax.nn.gelu(v, approximate=True), sums)
    activated = activated.astype(BF)
    ffn = scatter(mm(activated, wd, 1, 0).astype(BF), plane)
    out = turn_back((keep_own * (middle + ffn.astype(F32))).astype(BF))
    grad_act = mm(grad_all, wd, 1, 1)
    grad_up = pull(grad_act)[0].astype(BF)
    d_down = scatter(mm(activated, grad_all, 0, 0).astype(BF), "row")
    d_up = scatter(mm(grad_up, two, 0, 0).astype(BF), "row")
    e_two = scatter(mm(grad_up, wu, 1, 0).astype(BF), plane).astype(F32)
    normed2 = (middle - centre2) * inverse2
    back_two, g_gain2, g_bias2 = norm_backward(e_two, normed2, inverse2, gain2, keep_own)
    grad_middle = grad_own.astype(F32) + back_two
    grad_attn = gather(grad_middle.astype(BF), "col")
    grad_att = mm(grad_attn, wo, 1, 1).astype(BF)
    d_out = scatter(mm(attended, grad_attn, 0, 0).astype(BF), "row")
    dq, dkv = attend_back(queries, kv, lengths, row * t, logs, grad_att.reshape(b, t, -1))
    dq = dq.reshape(m, -1)
    dkv = dkv.reshape(b, nr, t, 2 * hd).transpose(1, 0, 2, 3).reshape(nr * m, 2 * hd)
    dkv_own = scatter(dkv, ("row", "col"))
    d_query = scatter(mm(dq, one, 0, 0).astype(BF), "row")
    e_one = scatter(mm(dq, wq, 1, 0).astype(BF), "col").astype(F32) + mm(dkv_own, wkv, 1, 1)
    normed1 = (x_own - mine(centre)) * mine(inverse)
    back_one, g_gain1, g_bias1 = norm_backward(e_one, normed1, mine(inverse), gain1, keep_own)
    grad_in = turn_back((grad_middle + back_one).astype(BF))
    d_kv = scatter(mm(one_own, dkv_own, 0, 0).astype(BF), "col")
    d_kv = lax.psum(d_kv, ("dp", "row")).astype(F32)
    small = lax.psum(jnp.stack([g_gain1, g_bias1, g_gain2, g_bias2]), ("dp", "row", "col"))
    small = lax.dynamic_slice_in_dim(small, col * f, f, 1)
    d_query = lax.psum(turn_back(d_query), "dp").astype(F32).T
    d_out = lax.psum(turn_back(d_out), "dp").astype(F32)
    d_up = gather(turn_back(d_up), "dp").astype(F32).T
    d_down = gather(turn_back(d_down), "dp").astype(F32)
    return (
        out.reshape(b, t, f),
        grad_in.reshape(b, t, f),
        small[0],
        small[1],
        d_query,
        d_kv,
        d_out,
        small[2],
        small[3],
        d_up,
        d_down,
    )


def solution(mesh):
    act, vec = (P("dp", "row", "col"), P("col"))
    wide, tall = (P("col", "row"), P("row", "col"))
    return jax.shard_map(
        local,
        mesh=mesh,
        in_specs=(act, P("dp"), act, vec, vec, wide, P("col", None), tall, vec, vec, wide, tall),
        out_specs=(act, act, vec, vec, wide, P("col", None), tall, vec, vec, wide, tall),
        check_vma=False,
    )
```

profile of v0, /device:TPU:0, one launch (start us, length us, event | category | flops | bytes accessed | tf_op | source)
XLA Modules:
  0.0 1477.3 jit_solution(9713727474657189356)
XLA Ops:
  10.0 13.0 all_to_all.200
  24.2 5.3 all_gather.40
  29.6 17.6 %all-gather.13.cloned.1.call-done = bf16[1024,2048]{1,0:T(8,128)(2,1)} async-done(((bf16[1024,512]{1,0:T(8,128)(2,1)}), bf16[1024,2048]{1,0:T(8,128)(2,1)}) %all-gather.13.cloned.1.call-update) | async-done | bytes 4194320 | tf_op jit(solution)/shard_map/all_gather | solution.py:43
  47.2 3.6 convert_reduce_fusion
  50.8 7.5 fusion.11
  58.3 7.5 all-gather.17.cloned.1.call-done
  68.4 3.5 all-to-all-start.1
  73.9 6.9 all-to-all-done.1
  82.3 31.9 %all-gather.15.cloned.1.call-done = bf16[512,2048]{0,1:T(8,128)(2,1)} async-done(((bf16[128,2048]{0,1:T(8,128)(2,1)}), bf16[512,2048]{0,1:T(8,128)(2,1)}) %all-gather.15.cloned.1.call-update) | async-done | bytes 2097168 | tf_op jit(solution)/shard_map/all_gather | solution.py:43
  114.2 5.2 convolution_convert_fusion.10
  119.4 37.1 %all-gather.19.cloned.1.call-done = bf16[4096,256]{1,0:T(8,128)(2,1)} async-done(((bf16[256,256]{1,0:T(8,128)(2,1)}), bf16[4096,256]{1,0:T(8,128)(2,1)}) %all-gather.19.cloned.1.call-update) | async-done | bytes 2097168 | tf_op jit(solution)/shard_map/all_gather | solution.py:43
  184.7 18.8 %all-gather.21.cloned.1.call-done = bf16[512,2048]{0,1:T(8,128)(2,1)} async-done(((bf16[128,2048]{0,1:T(8,128)(2,1)}), bf16[512,2048]{0,1:T(8,128)(2,1)}) %all-gather.21.cloned.1.call-update) | async-done | bytes 2097168 | tf_op jit(solution)/shard_map/all_gather | solution.py:43
  203.5 6.3 convolution_convert_fusion.5
  210.0 17.2 %all_to_all.201 = bf16[4,256,512]{2,1,0:T(8,128)(2,1)S(1)} all-to-all(bf16[4,256,512]{2,1,0:T(8,128)(2,1)S(1)} %bitcast.406), channel_id=1, replica_groups=mesh['dp'=2,'row'=4,'col'=4] {'col'}, dimensions={0} | all-to-all | bytes 2097152 | tf_op jit(solution)/shard_map/all_to_all | solution.py:35
  229.1 28.4 %all_to_all.202 = bf16[4,256,512]{2,1,0:T(8,128)(2,1)S(1)} all-to-all(bf16[4,256,512]{2,1,0:T(8,128)(2,1)S(1)} %fusion.58), channel_id=1, replica_groups=mesh['dp'=2,'row'=4,'col'=4] {'col'}, dimensions={0} | all-to-all | bytes 2097152 | tf_op jit(solution)/shard_map/all_to_all | solution.py:35
  260.6 16.9 %all_to_all.203 = bf16[4,256,512]{2,1,0:T(8,128)(2,1)S(1)} all-to-all(bf16[4,256,512]{2,1,0:T(8,128)(2,1)S(1)} %bitcast.413), channel_id=1, replica_groups=mesh['dp'=2,'row'=4,'col'=4] {'col'}, dimensions={0} | all-to-all | bytes 2097152 | tf_op jit(solution)/shard_map/all_to_all | solution.py:35
  281.1 3.7 multiply_convert_fusion.10
  284.8 62.0 %all-gather.27.cloned.1.call-done = bf16[1024,2048]{0,1:T(8,128)(2,1)} async-done(((bf16[256,2048]{0,1:T(8,128)(2,1)}), bf16[1024,2048]{0,1:T(8,128)(2,1)}) %all-gather.27.cloned.1.call-update) | async-done | bytes 4194320 | tf_op jit(solution)/shard_map/all_gather | solution.py:43
  346.8 55.2 %all-gather.29.cloned.1.call-done = bf16[2048,2048]{1,0:T(8,128)(2,1)} async-done(((bf16[256,2048]{1,0:T(8,128)(2,1)}), bf16[2048,2048]{1,0:T(8,128)(2,1)}) %all-gather.29.cloned.1.call-update) | async-done | bytes 8388624 | tf_op jit(solution)/shard_map/all_gather | solution.py:43
  402.0 14.5 fusion.125
  416.4 67.8 %all-gather.25.cloned.1.call-done = bf16[1024,2048]{0,1:T(8,128)(2,1)} async-done(((bf16[256,2048]{0,1:T(8,128)(2,1)}), bf16[1024,2048]{0,1:T(8,128)(2,1)}) %all-gather.25.cloned.1.call-update) | async-done | bytes 4194320 | tf_op jit(solution)/shard_map/all_gather | solution.py:43
  484.2 55.1 %all-gather.23.cloned.1.call-done = bf16[2048,2048]{1,0:T(8,128)(2,1)} async-done(((bf16[256,2048]{1,0:T(8,128)(2,1)}), bf16[2048,2048]{1,0:T(8,128)(2,1)}) %all-gather.23.cloned.1.call-update) | async-done | bytes 8388624 | tf_op jit(solution)/shard_map/all_gather | solution.py:43
  539.3 22.2 %fusion.6 = (bf16[2048,1024]{1,0:T(8,128)(2,1)S(1)}, f32[2048,1024]{1,0:T(8,128)}) fusion(f32[2048,1024]{1,0:T(8,128)} %fusion.125, bf16[2048,2048]{1,0:T(8,128)(2,1)} %all-gather.23.cloned.1.call-done, bf16[1024,2048]{0,1:T(8,128)(2,1)} %all-gather.25.cloned.1.call-done), kind=kOutput, calls=%fused_computation.11 | convolution fusion | flops 8631877632 | bytes 33554432 | tf_op jit(solution)/shard_map/dot_general | solution.py:12
  563.5 11.0 convolution_convert_fusion
  574.5 15.4 %convolution_convert_fusion.1 = bf16[2048,2048]{1,0:T(8,128)(2,1)} fusion(bf16[1024,2048]{0,1:T(8,128)(2,1)} %all-gather.27.cloned.1.call-done, f32[2048,1024]{1,0:T(8,128)} %get-tuple-element.69), kind=kOutput, calls=%fused_computation.20 | convolution fusion | flops 8613003264 | bytes 20971520 | tf_op jit(solution)/shard_map/dot_general | solution.py:12
  590.0 55.9 %reduce-scatter.15.cloned.1.call-done = bf16[256,2048]{1,0:T(8,128)(2,1)} async-done(((bf16[2048,2048]{1,0:T(8,128)(2,1)}), bf16[256,2048]{1,0:T(8,128)(2,1)}) %reduce-scatter.15.cloned.1.call-update) | async-done | bytes 1048592 | tf_op jit(solution)/shard_map/reduce_scatter | solution.py:47
  648.7 71.8 %reduce-scatter.13.cloned.1.call-done = bf16[256,2048]{1,0:T(8,128)(2,1)} async-done(((bf16[2048,2048]{1,0:T(8,128)(2,1)}), bf16[256,2048]{1,0:T(8,128)(2,1)}) %reduce-scatter.13.cloned.1.call-update) | async-done | bytes 1048592 | tf_op jit(solution)/shard_map/reduce_scatter | solution.py:47
  720.5 5.3 fusion.111
  725.9 34.5 %all-gather.31.cloned.1.call-done = bf16[1024,2048]{1,0:T(8,128)(2,1)} async-done(((bf16[256,2048]{1,0:T(8,128)(2,1)}), bf16[1024,2048]{1,0:T(8,128)(2,1)}) %all-gather.31.cloned.1.call-update) | async-done | bytes 4194320 | tf_op jit(solution)/shard_map/all_gather | solution.py:43
  760.4 5.3 convolution_convert_fusion.9
  767.4 2.9 multiply_reduce_fusion.3
  774.3 3.0 multiply_reduce_fusion.2
  799.9 2.9 multiply_reduce_fusion.4
  804.8 4.4 multiply_convert_fusion.4
  812.1 4.4 multiply_convert_fusion.8
  818.9 3.1 multiply_convert_fusion.1
  822.0 3.8 multiply_convert_fusion.2
  825.8 3.8 multiply_convert_fusion.3
  849.0 16.0 %convolution_convert_fusion.2 = bf16[1024,2048]{1,0:T(8,128)(2,1)} fusion(bf16[2048,2048]{1,0:T(8,128)(2,1)} %all-gather.29.cloned.1.call-done, f32[2048,1024]{1,0:T(8,128)} %get-tuple-element.69), kind=kOutput, calls=%fused_computation.73 | convolution fusion | flops 8610906112 | bytes 20971520 | tf_op jit(solution)/shard_map/dot_general | solution.py:12
  865.3 14.2 convolution_convert_fusion.3
  892.1 6.0 convolution_convert_fusion.7
  898.5 5.9 convolution_convert_fusion.6
  904.4 6.3 reduce-scatter.19.cloned.1.call-done
  913.4 75.8 %reduce-scatter.29.cloned.1.call-done = bf16[256,2048]{1,0:T(8,128)(2,1)} async-done(((bf16[1024,2048]{1,0:T(8,128)(2,1)}), bf16[256,2048]{1,0:T(8,128)(2,1)}) %reduce-scatter.29.cloned.1.call-update) | async-done | bytes 1048592 | tf_op jit(solution)/shard_map/reduce_scatter | solution.py:47
  990.5 17.6 %all_to_all.204 = bf16[256,4,512]{2,0,1:T(8,128)(2,1)} all-to-all(bf16[256,4,512]{2,0,1:T(8,128)(2,1)S(1)} %bitcast.415), channel_id=1, replica_groups=mesh['dp'=2,'row'=4,'col'=4] {'col'}, dimensions={1} | all-to-all | bytes 2097152 | tf_op jit(solution)/shard_map/all_to_all | solution.py:39
  1008.2 6.0 convolution_convert_fusion.4
  1014.3 54.5 %reduce-scatter.27.cloned.1.call-done = bf16[256,2048]{1,0:T(8,128)(2,1)} async-done(((bf16[1024,2048]{1,0:T(8,128)(2,1)}), bf16[256,2048]{1,0:T(8,128)(2,1)}) %reduce-scatter.27.cloned.1.call-update) | async-done | bytes 1048592 | tf_op jit(solution)/shard_map/reduce_scatter | solution.py:47
  1070.1 17.0 %all_to_all.205 = bf16[256,4,512]{2,0,1:T(8,128)(2,1)S(1)} all-to-all(bf16[256,4,512]{2,0,1:T(8,128)(2,1)S(1)} %bitcast.416), channel_id=1, replica_groups=mesh['dp'=2,'row'=4,'col'=4] {'col'}, dimensions={1} | all-to-all | bytes 2097152 | tf_op jit(solution)/shard_map/all_to_all | solution.py:39
  1088.5 26.9 %reduce-scatter.21.cloned.1.call-done = bf16[128,2048]{1,0:T(8,128)(2,1)} async-done(((bf16[512,2048]{1,0:T(8,128)(2,1)}), bf16[128,2048]{1,0:T(8,128)(2,1)}) %reduce-scatter.21.cloned.1.call-update) | async-done | bytes 524304 | tf_op jit(solution)/shard_map/reduce_scatter | solution.py:47
  1117.2 3.5 all-to-all-start.7
  1120.7 40.1 %reduce-scatter.25.cloned.1.call-done = bf16[128,2048]{1,0:T(8,128)(2,1)} async-done(((bf16[512,2048]{1,0:T(8,128)(2,1)}), bf16[128,2048]{1,0:T(8,128)(2,1)}) %reduce-scatter.25.cloned.1.call-update) | async-done | bytes 524304 | tf_op jit(solution)/shard_map/reduce_scatter | solution.py:47
  1162.8 3.5 all-to-all-start.8
  1166.3 21.8 %reduce-scatter.23.cloned.1.call-done = bf16[512,256]{1,0:T(8,128)(2,1)} async-done(((bf16[2048,256]{1,0:T(8,128)(2,1)}), bf16[512,256]{1,0:T(8,128)(2,1)}) %reduce-scatter.23.cloned.1.call-update) | async-done | bytes 262160 | tf_op jit(solution)/shard_map/reduce_scatter | solution.py:47
  1189.6 33.1 %all-gather.35.cloned.1.call-done = bf16[2048,512]{1,0:T(8,128)(2,1)} async-done(((bf16[1024,512]{1,0:T(8,128)(2,1)}), bf16[2048,512]{1,0:T(8,128)(2,1)}) %all-gather.35.cloned.1.call-update) | async-done | bytes 2097168 | tf_op jit(solution)/shard_map/all_gather | solution.py:43
  1222.7 4.2 convert_element_type.337
  1229.0 3.6 all-to-all-start.4
  1233.2 37.7 %reduce-scatter.17.cloned.1.call-done = bf16[256,2048]{1,0:T(8,128)(2,1)} async-done(((bf16[1024,2048]{1,0:T(8,128)(2,1)}), bf16[256,2048]{1,0:T(8,128)(2,1)}) %reduce-scatter.17.cloned.1.call-update) | async-done | bytes 1048592 | tf_op jit(solution)/shard_map/reduce_scatter | solution.py:47
  1270.9 3.1 fusion.39
  1277.1 4.3 all-to-all-start.6
  1281.4 24.4 %all-gather.33.cloned.1.call-done = bf16[2048,512]{0,1:T(8,128)(2,1)} async-done(((bf16[1024,512]{0,1:T(8,128)(2,1)}), bf16[2048,512]{0,1:T(8,128)(2,1)}) %all-gather.33.cloned.1.call-update) | async-done | bytes 2097168 | tf_op jit(solution)/shard_map/all_gather | solution.py:43
  1305.8 4.3 convert_bitcast_fusion
  1310.1 69.8 %all-reduce.4.cloned.1.call-done = bf16[512,256]{1,0:T(8,128)(2,1)} async-done(((bf16[512,256]{1,0:T(8,128)(2,1)}), bf16[512,256]{1,0:T(8,128)(2,1)}) %all-reduce.4.cloned.1.call-update) | async-done | bytes 262160 | tf_op jit(solution)/shard_map/psum | solution.py:185
  1381.6 40.7 %all-reduce.6.cloned.1.call-done = (bf16[512,512]{1,0:T(8,128)(2,1)}, bf16[512,512]{1,0:T(8,128)(2,1)}) async-done(((bf16[512,512]{1,0:T(8,128)(2,1)}, bf16[512,512]{1,0:T(8,128)(2,1)}), (bf16[512,512]{1,0:T(8,128)(2,1)}, bf16[512,512]{1,0:T(8,128)(2,1)})) %all-reduce.6.cloned.1.call-update) | async-done | bytes 1048592 | tf_op jit(solution)/shard_map/psum | solution.py:188
  1426.6 39.5 %psum.28 = f32[4,2048]{1,0:T(4,128)S(1)} all-reduce(f32[4,2048]{1,0:T(4,128)S(1)} %pad_maximum_fusion.2), channel_id=1, replica_groups=mesh['dp'=2,'row'=4,'col'=4] {'dp','row','col'}, use_global_device_ids=true, to_apply=%region_41.42 | all-reduce | flops 8192 | bytes 65536 | tf_op jit(solution)/shard_map/psum | solution.py:186
  (304 shorter events, 147.1 us)
Async XLA Ops:
  7.2 202.7 %copy-start = (bf16[2048,512]{1,0:T(8,128)(2,1)S(1)}, bf16[2048,512]{1,0:T(8,128)(2,1)}, u32[]{:S(2)}) copy-start(bf16[2048,512]{1,0:T(8,128)(2,1)} %param.23) | copy-start | bytes 6291460
  7.2 16.9 %copy-start.53 = (s32[2]{0:T(128)S(1)}, s32[2]{0:T(128)}, u32[]{:S(2)}) copy-start(s32[2]{0:T(128)} %param.13) | copy-start | bytes 28
  7.2 17.0 %copy-start.54 = (f32[512]{0:T(512)S(1)}, f32[512]{0:T(512)}, u32[]{:S(2)}) copy-start(f32[512]{0:T(512)} %param.21) | copy-start | bytes 6148
  7.2 17.0 %copy-start.55 = (f32[512]{0:T(512)S(1)}, f32[512]{0:T(512)}, u32[]{:S(2)}) copy-start(f32[512]{0:T(512)} %param.20) | copy-start | bytes 6148
  7.2 17.0 %copy-start.56 = (f32[512]{0:T(512)S(1)}, f32[512]{0:T(512)}, u32[]{:S(2)}) copy-start(f32[512]{0:T(512)} %param.16) | copy-start | bytes 6148
  7.2 17.0 %copy-start.57 = (f32[512]{0:T(512)S(1)}, f32[512]{0:T(512)}, u32[]{:S(2)}) copy-start(f32[512]{0:T(512)} %param.15) | copy-start | bytes 6148
  7.2 39.9 %all-gather.13.cloned.1.call-start = ((), (), s32[]{:S(2)}) async-start(), calls=%async_computation.21 | async-start | bytes 5242880 | tf_op jit(solution)/shard_map/all_gather | solution.py:43
  8.0 57.8 %all-gather.17.cloned.1.call-start = ((), (), s32[]{:S(2)}) async-start(), calls=%async_computation.23 | async-start | bytes 1310720 | tf_op jit(solution)/shard_map/all_gather | solution.py:43
  8.7 105.5 %all-gather.15.cloned.1.call-start = ((), (), s32[]{:S(2)}) async-start(), calls=%async_computation.22 | async-start | bytes 2621440 | tf_op jit(solution)/shard_map/all_gather | solution.py:43
  24.0 132.5 %all-gather.19.cloned.1.call-start = ((), (), s32[]{:S(2)}) async-start(), calls=%async_computation.24 | async-start | bytes 2228224 | tf_op jit(solution)/shard_map/all_gather | solution.py:43
  29.6 28.7 %copy-start.49 = (f32[1,2048]{1,0:T(1,128)}, f32[1,2048]{1,0:T(1,128)S(1)}, u32[]{:S(2)}) copy-start(f32[1,2048]{1,0:T(1,128)S(1)} %get-tuple-element.32) | copy-start | bytes 24580
  50.8 7.5 copy-start.51
  50.8 7.5 copy-start.52
  68.4 12.3 all-to-all-start.1
  71.9 131.5 %all-gather.21.cloned.1.call-start = ((), (), s32[]{:S(2)}) async-start(), calls=%async_computation.25 | async-start | bytes 2621440 | tf_op jit(solution)/shard_map/all_gather | solution.py:43
  81.8 197.1 %reduce-scatter.11.cloned.1.call-start = ((), (), s32[]{:S(2)}) async-start(), calls=%async_computation.26 | async-start | bytes 5242880 | tf_op jit(solution)/shard_map/reduce_scatter | solution.py:47
  119.4 48.5 %copy-start.47 = (bf16[1024,512]{1,0:T(8,128)(2,1)}, bf16[1024,512]{1,0:T(8,128)(2,1)S(1)}, u32[]{:S(2)}) copy-start(bf16[1024,512]{1,0:T(8,128)(2,1)S(1)} %convolution_convert_fusion.10) | copy-start | bytes 3145732
  158.2 23.6 %copy-start.19 = (bf16[4,2,512,256]{3,2,0,1:T(8,128)(2,1)}, bf16[4,2,512,256]{3,2,0,1:T(8,128)(2,1)S(1)}, u32[]{:S(2)}) copy-start(bf16[4,2,512,256]{3,2,0,1:T(8,128)(2,1)S(1)} %copy.68) | copy-start | bytes 6291460
  159.6 15.7 %copy-start.12 = (f32[512,2048]{1,0:T(8,128)}, f32[512,2048]{1,0:T(8,128)S(1)}, u32[]{:S(2)}) copy-start(f32[512,2048]{1,0:T(8,128)S(1)} %get-tuple-element.53) | copy-start | bytes 12582916
  161.0 15.2 %copy-start.10 = (f32[512,2048]{1,0:T(8,128)}, f32[512,2048]{1,0:T(8,128)S(1)}, u32[]{:S(2)}) copy-start(f32[512,2048]{1,0:T(8,128)S(1)} %get-tuple-element.55) | copy-start | bytes 12582916
  162.4 14.8 copy-start.8
  163.8 14.3 copy-start.14
  165.2 13.8 copy-start.6
  166.5 13.4 copy-start.4
  167.9 12.9 copy-start.2
  169.5 12.3 copy-start.16
  209.8 19.0 %copy-start.45 = (bf16[2,512,512]{2,1,0:T(8,128)(2,1)S(1)}, bf16[2,512,512]{2,1,0:T(8,128)(2,1)}, u32[]{:S(2)}) copy-start(bf16[2,512,512]{2,1,0:T(8,128)(2,1)} %param.14) | copy-start | bytes 3145732
  209.8 136.9 %all-gather.27.cloned.1.call-start = ((), (), s32[]{:S(2)}) async-start(), calls=%async_computation.29 | async-start | bytes 5242880 | tf_op jit(solution)/shard_map/all_gather | solution.py:43
  228.5 173.5 %all-gather.29.cloned.1.call-start = ((), (), s32[]{:S(2)}) async-start(), calls=%async_computation.31 | async-start | bytes 9437184 | tf_op jit(solution)/shard_map/all_gather | solution.py:43
  258.7 225.6 %all-gather.25.cloned.1.call-start = ((), (), s32[]{:S(2)}) async-start(), calls=%async_computation.28 | async-start | bytes 5242880 | tf_op jit(solution)/shard_map/all_gather | solution.py:43
  278.8 260.5 %all-gather.23.cloned.1.call-start = ((), (), s32[]{:S(2)}) async-start(), calls=%async_computation.27 | async-start | bytes 9437184 | tf_op jit(solution)/shard_map/all_gather | solution.py:43
  284.7 361.2 %reduce-scatter.15.cloned.1.call-start = ((), (), s32[]{:S(2)}) async-start(), calls=%async_computation.32 | async-start | bytes 9437184 | tf_op jit(solution)/shard_map/reduce_scatter | solution.py:47
  539.3 24.1 %copy-start.58 = (bf16[1024,2048]{0,1:T(8,128)(2,1)S(1)}, bf16[1024,2048]{0,1:T(8,128)(2,1)}, u32[]{:S(2)}) copy-start(bf16[1024,2048]{0,1:T(8,128)(2,1)} %all-gather.25.cloned.1.call-done) | copy-start | bytes 12582916
  574.5 146.1 %reduce-scatter.13.cloned.1.call-start = ((), (), s32[]{:S(2)}) async-start(), calls=%async_computation.30 | async-start | bytes 9437184 | tf_op jit(solution)/shard_map/reduce_scatter | solution.py:47
  589.9 56.0 %copy-start.38 = (bf16[256,2048]{1,0:T(8,128)(2,1)S(1)}, bf16[256,2048]{1,0:T(8,128)(2,1)}, u32[]{:S(2)}) copy-start(bf16[256,2048]{1,0:T(8,128)(2,1)} %reduce-scatter.11.cloned.1.call-done) | copy-start | bytes 3145732
  589.9 130.6 %copy-start.39 = (bf16[4,32,8,512]{3,2,0,1:T(8,128)(2,1)S(1)}, bf16[4,32,8,512]{3,2,0,1:T(8,128)(2,1)}, u32[]{:S(2)}) copy-start(bf16[4,32,8,512]{3,2,0,1:T(8,128)(2,1)} %copy.95) | copy-start | bytes 3145732
  589.9 170.5 %all-gather.31.cloned.1.call-start = ((), (), s32[]{:S(2)}) async-start(), calls=%async_computation.33 | async-start | bytes 5242880 | tf_op jit(solution)/shard_map/all_gather | solution.py:43
  725.8 184.9 %reduce-scatter.19.cloned.1.call-start = ((), (), s32[]{:S(2)}) async-start(), calls=%async_computation.35 | async-start | bytes 2228224 | tf_op jit(solution)/shard_map/reduce_scatter | solution.py:47
  760.4 5.3 copy-start.15
  822.0 11.4 copy-start.25
  825.8 5.7 copy-start.26
  836.2 9.4 copy-start.29
  849.0 140.3 %reduce-scatter.29.cloned.1.call-start = ((), (), s32[]{:S(2)}) async-start(), calls=%async_computation.42 | async-start | bytes 5242880 | tf_op jit(solution)/shard_map/reduce_scatter | solution.py:47
  865.0 203.8 %reduce-scatter.27.cloned.1.call-start = ((), (), s32[]{:S(2)}) async-start(), calls=%async_computation.40 | async-start | bytes 5242880 | tf_op jit(solution)/shard_map/reduce_scatter | solution.py:47
  879.6 235.8 %reduce-scatter.21.cloned.1.call-start = ((), (), s32[]{:S(2)}) async-start(), calls=%async_computation.36 | async-start | bytes 2621440 | tf_op jit(solution)/shard_map/reduce_scatter | solution.py:47
  881.1 5.2 copy-start.28
  881.1 6.0 copy-start.24
  892.1 6.3 copy-start.46
  898.1 262.6 %reduce-scatter.25.cloned.1.call-start = ((), (), s32[]{:S(2)}) async-start(), calls=%async_computation.39 | async-start | bytes 2621440 | tf_op jit(solution)/shard_map/reduce_scatter | solution.py:47
  904.3 283.8 %reduce-scatter.23.cloned.1.call-start = ((), (), s32[]{:S(2)}) async-start(), calls=%async_computation.37 | async-start | bytes 1310720 | tf_op jit(solution)/shard_map/reduce_scatter | solution.py:47
  913.4 309.3 %all-gather.35.cloned.1.call-start = ((), (), s32[]{:S(2)}) async-start(), calls=%async_computation.43 | async-start | bytes 3145728 | tf_op jit(solution)/shard_map/all_gather | solution.py:43
  1008.2 262.7 %reduce-scatter.17.cloned.1.call-start = ((), (), s32[]{:S(2)}) async-start(), calls=%async_computation.34 | async-start | bytes 5242880 | tf_op jit(solution)/shard_map/reduce_scatter | solution.py:47
  1014.2 291.6 %all-gather.33.cloned.1.call-start = ((), (), s32[]{:S(2)}) async-start(), calls=%async_computation.41 | async-start | bytes 3145728 | tf_op jit(solution)/shard_map/all_gather | solution.py:43
  1117.2 45.6 %all-to-all-start.7 = ((bf16[128,4,512]{2,0,1:T(8,128)(2,1)}), bf16[128,4,512]{2,0,1:T(8,128)(2,1)S(1)}, u32[]{:S(2)}, u32[]{:S(2)}) async-start(bf16[128,4,512]{2,0,1:T(8,128)(2,1)} %bitcast.354), calls=%async_computation.13 | async-start | bytes 1048576 | tf_op jit(solution)/shard_map/all_to_all | solution.py:39
  1160.8 66.1 %copy-start.41 = (bf16[256,2048]{1,0:T(8,128)(2,1)S(1)}, bf16[256,2048]{1,0:T(8,128)(2,1)}, u32[]{:S(2)}) copy-start(bf16[256,2048]{1,0:T(8,128)(2,1)} %get-tuple-element.27) | copy-start | bytes 3145732
  1162.8 66.2 %all-to-all-start.8 = ((bf16[128,4,512]{2,0,1:T(8,128)(2,1)}), bf16[128,4,512]{2,0,1:T(8,128)(2,1)S(1)}, u32[]{:S(2)}, u32[]{:S(2)}) async-start(bf16[128,4,512]{2,0,1:T(8,128)(2,1)} %bitcast.353), calls=%async_computation.16 | async-start | bytes 1048576 | tf_op jit(solution)/shard_map/all_to_all | solution.py:39
  1166.2 213.6 %all-reduce.4.cloned.1.call-start = ((), (), s32[]{:S(2)}) async-start(), calls=%async_computation.38 | async-start | bytes 524288 | tf_op jit(solution)/shard_map/psum | solution.py:185
  1226.9 44.0 %copy-start.48 = (bf16[256,256]{1,0:T(8,128)(2,1)S(1)}, bf16[256,256]{1,0:T(8,128)(2,1)}, u32[]{:S(2)}) copy-start(bf16[256,256]{1,0:T(8,128)(2,1)} %reduce-scatter.19.cloned.1.call-done) | copy-start | bytes 393220
  1226.9 44.0 %copy-start.50 = (f32[1,2048]{1,0:T(1,128)S(1)}, f32[1,2048]{1,0:T(1,128)}, u32[]{:S(2)}) copy-start(f32[1,2048]{1,0:T(1,128)} %copy-done.49) | copy-start | bytes 24580
  1229.0 48.1 %all-to-all-start.4 = ((bf16[256,4,512]{2,0,1:T(8,128)(2,1)}), bf16[256,4,512]{2,0,1:T(8,128)(2,1)S(1)}, u32[]{:S(2)}, u32[]{:S(2)}) async-start(bf16[256,4,512]{2,0,1:T(8,128)(2,1)} %bitcast.352), calls=%async_computation.6 | async-start | bytes 2097152 | tf_op jit(solution)/shard_map/all_to_all | solution.py:39
  1232.6 189.7 %all-reduce.6.cloned.1.call-start = ((), (), s32[]{:S(2)}) async-start(), calls=%async_computation.44 | async-start | bytes 2097152 | tf_op jit(solution)/shard_map/psum | solution.py:188
  1232.7 41.3 %copy-start.40 = (f32[256,2048]{1,0:T(8,128)S(1)}, f32[256,2048]{1,0:T(8,128)}, u32[]{:S(2)}) copy-start(f32[256,2048]{1,0:T(8,128)} %get-tuple-element.26) | copy-start | bytes 6291460
  1277.1 189.7 %all-to-all-start.6 = ((bf16[256,4,512]{2,0,1:T(8,128)(2,1)}), bf16[256,4,512]{2,0,1:T(8,128)(2,1)}, u32[]{:S(2)}, u32[]{:S(2)}) async-start(bf16[256,4,512]{2,0,1:T(8,128)(2,1)} %bitcast.351), calls=%async_computation.11 | async-start | bytes 2097152 | tf_op jit(solution)/shard_map/all_to_all | solution.py:39
  1305.8 164.3 %copy-start.1 = (bf16[2048,512]{1,0:T(8,128)(2,1)S(1)}, bf16[2048,512]{1,0:T(8,128)(2,1)}, u32[]{:S(2)}) copy-start(bf16[2048,512]{1,0:T(8,128)(2,1)} %param.23) | copy-start | bytes 6291460
  (25 other events, 72.8 us)
Sparse Core Ops, SparseCore 0:
  9.6 37.4 all-gather.12
  48.7 17.0 all-gather.16
  67.9 46.2 all-gather.14
  116.8 39.6 all-gather.18
  158.4 44.9 all-gather.20
  209.9 53.9 reduce-scatter.10
  266.2 80.5 all-gather.26
  349.4 52.5 all-gather.28
  403.6 80.5 all-gather.24
  486.7 52.5 all-gather.22
  574.6 71.3 reduce-scatter.14
  649.2 71.2 reduce-scatter.12
  725.9 34.4 all-gather.30
  849.1 61.5 reduce-scatter.18
  913.4 75.7 reduce-scatter.28
  991.5 77.2 reduce-scatter.26
  1070.9 44.3 reduce-scatter.20
  1117.6 43.1 reduce-scatter.24
  1163.9 24.1 reduce-scatter.22
  1189.6 33.1 all-gather.34
  1226.0 44.8 reduce-scatter.16
  1273.0 32.7 all-gather.32
  1309.2 70.6 all-reduce.3
  1382.7 39.5 all-reduce.5
where the time goes:
time: 1480 us
  waiting for transfers between devices  955 us (65%)
  matrix products  214 us (14%)
  blocking collectives  155 us (10%)
  other arithmetic  73.4 us (5%)
  local copies, waits for them, and re-layouts  43.2 us (3%)
  starting transfers between devices  20.2 us (1%)
  between operations  16 us (1%)
    all_gather x12, waiting for transfers between devices, gather(): return lax.all_gather(x, axes, axis=dim, tiled=True)  445 us
    reduce_scatter x10, waiting for transfers between devices, scatter(): return lax.psum_scatter(x, axes, scatter_dimension=0, tiled=True)  391 us
    dot_general x63, matrix products, mm(): lax.dot_general(a, b, (((ca,), (cb,)), ((), ())), preferred_element_type=...  214 us
    all_to_all x4, blocking collectives, turn(): return lax.all_to_all(weight, 'col', 0, 1, tiled=True)  75.5 us
    psum x1, waiting for transfers between devices, local(): d_kv = lax.psum(d_kv, ('dp', 'row')).astype(F32)  69.8 us
    psum x1, waiting for transfers between devices, local(): d_query = lax.psum(turn_back(d_query), 'dp').astype(F32).T  40.7 us
    psum x1, blocking collectives, local(): lax.psum(jnp.stack([g_gain1, g_bias1, g_gain2, g_bias2]), ('dp', 'row', '...  39.5 us
    all_to_all x2, blocking collectives, turn_back(): return lax.all_to_all(rows, 'col', 1, 0, tiled=True)  34.6 us
  transfers between devices with their start and end apart: 29, of which 24 were waited for; matrix products, arithmetic and copies ran while one was open for 13% of the time, Pallas kernels for 0%

commit v1 on v0

--- a/solution.py
+++ b/solution.py
@@ -6,6 +6,13 @@
 eps = 1e-05
 BF = jnp.bfloat16
 F32 = jnp.float32
+
+
+def fill_hubs_up(across, mat):
+    block_now = jnp.stack(jnp.split(mat, lax.axis_size(across), 1), 0)
+    return jnp.concatenate(
+        lax.all_to_all(block_now, axis_name=across, concat_axis=0, split_axis=0), 0
+    )
 
 
 def mm(a, b, ca, cb):
@@ -36,7 +43,7 @@
 
 
 def turn_back(rows):
-    return lax.all_to_all(rows, "col", 1, 0, tiled=True)
+    return fill_hubs_up("col", rows)
 
 
 def gather(x, axes, dim=0):

time: 1480 us -> 1410 us (0.953)
  waiting for transfers between devices: 955 us -> 880 us
    reduce_scatter x10, waiting for transfers between devices: 391 us -> 331 us  [scatter(): return lax.psum_scatter(x, axes, scatter_dimension=0, tiled=True)]
    all_gather x12, waiting for transfers between devices: 445 us -> 423 us  [gather(): return lax.all_gather(x, axes, axis=dim, tiled=True)]
  transfers between devices with their start and end apart: 29 -> 29, of which waited for: 24 -> 24; matrix products, arithmetic and copies ran while one was open for 13% -> 20% of each run, Pallas kernels for 0% -> 0%
where the time goes in v1:
time: 1410 us
  waiting for transfers between devices  880 us (62%)
  matrix products  219 us (16%)
  blocking collectives  156 us (11%)
  other arithmetic  78.9 us (6%)
  local copies, waits for them, and re-layouts  35.6 us (3%)
  starting transfers between devices  20.2 us (1%)
  between operations  15.9 us (1%)
    all_gather x12, waiting for transfers between devices, gather(): return lax.all_gather(x, axes, axis=dim, tiled=True)  423 us
    reduce_scatter x10, waiting for transfers between devices, scatter(): return lax.psum_scatter(x, axes, scatter_dimension=0, tiled=True)  331 us
    dot_general x63, matrix products, mm(): lax.dot_general(a, b, (((ca,), (cb,)), ((), ())), preferred_element_type=...  219 us
    all_to_all x4, blocking collectives, turn(): return lax.all_to_all(weight, 'col', 0, 1, tiled=True)  75.5 us
    psum x1, waiting for transfers between devices, local(): d_kv = lax.psum(d_kv, ('dp', 'row')).astype(F32)  69.7 us
    psum x1, waiting for transfers between devices, local(): d_query = lax.psum(turn_back(d_query), 'dp').astype(F32).T  40.7 us
    psum x1, blocking collectives, local(): lax.psum(jnp.stack([g_gain1, g_bias1, g_gain2, g_bias2]), ('dp', 'row', '...  39.5 us
    all_to_all x2, blocking collectives, fill_hubs_up(): lax.all_to_all(block_now, axis_name=across, concat_axis=0, split_axis=0)  36.1 us
  transfers between devices with their start and end apart: 29, of which 24 were waited for; matrix products, arithmetic and copies ran while one was open for 20% of the time, Pallas kernels for 0%

profile of v1, /device:TPU:0, one launch (start us, length us, event | category | flops | bytes accessed | tf_op | source)
XLA Modules:
  0.0 1405.7 jit_solution(7785542995526260991)
XLA Ops:
  10.0 13.0 all_to_all.122
  24.2 5.3 all_gather.40
  29.6 17.6 %all-gather.13.cloned.1.call-done = bf16[1024,2048]{1,0:T(8,128)(2,1)} async-done(((bf16[1024,512]{1,0:T(8,128)(2,1)}), bf16[1024,2048]{1,0:T(8,128)(2,1)}) %all-gather.13.cloned.1.call-update) | async-done | bytes 4194320 | tf_op jit(solution)/shard_map/all_gather | solution.py:50
  47.2 3.6 convert_reduce_fusion
  50.8 7.5 fusion.11
  58.3 7.5 all-gather.17.cloned.1.call-done
  68.4 3.5 all-to-all-start.1
  73.9 6.9 all-to-all-done.1
  82.4 31.9 %all-gather.15.cloned.1.call-done = bf16[512,2048]{0,1:T(8,128)(2,1)} async-done(((bf16[128,2048]{0,1:T(8,128)(2,1)}), bf16[512,2048]{0,1:T(8,128)(2,1)}) %all-gather.15.cloned.1.call-update) | async-done | bytes 2097168 | tf_op jit(solution)/shard_map/all_gather | solution.py:50
  114.2 5.2 convolution_convert_fusion.10
  119.4 37.0 %all-gather.19.cloned.1.call-done = bf16[4096,256]{1,0:T(8,128)(2,1)} async-done(((bf16[256,256]{1,0:T(8,128)(2,1)}), bf16[4096,256]{1,0:T(8,128)(2,1)}) %all-gather.19.cloned.1.call-update) | async-done | bytes 2097168 | tf_op jit(solution)/shard_map/all_gather | solution.py:50
  184.7 18.8 %all-gather.21.cloned.1.call-done = bf16[512,2048]{0,1:T(8,128)(2,1)} async-done(((bf16[128,2048]{0,1:T(8,128)(2,1)}), bf16[512,2048]{0,1:T(8,128)(2,1)}) %all-gather.21.cloned.1.call-update) | async-done | bytes 2097168 | tf_op jit(solution)/shard_map/all_gather | solution.py:50
  203.5 6.3 convolution_convert_fusion.5
  210.0 17.2 %all_to_all.123 = bf16[4,256,512]{2,1,0:T(8,128)(2,1)S(1)} all-to-all(bf16[4,256,512]{2,1,0:T(8,128)(2,1)S(1)} %bitcast.418), channel_id=1, replica_groups=mesh['dp'=2,'row'=4,'col'=4] {'col'}, dimensions={0} | all-to-all | bytes 2097152 | tf_op jit(solution)/shard_map/all_to_all | solution.py:42
  229.1 28.4 %all_to_all.124 = bf16[4,256,512]{2,1,0:T(8,128)(2,1)S(1)} all-to-all(bf16[4,256,512]{2,1,0:T(8,128)(2,1)S(1)} %fusion.58), channel_id=1, replica_groups=mesh['dp'=2,'row'=4,'col'=4] {'col'}, dimensions={0} | all-to-all | bytes 2097152 | tf_op jit(solution)/shard_map/all_to_all | solution.py:42
  260.6 16.9 %all_to_all.125 = bf16[4,256,512]{2,1,0:T(8,128)(2,1)S(1)} all-to-all(bf16[4,256,512]{2,1,0:T(8,128)(2,1)S(1)} %bitcast.425), channel_id=1, replica_groups=mesh['dp'=2,'row'=4,'col'=4] {'col'}, dimensions={0} | all-to-all | bytes 2097152 | tf_op jit(solution)/shard_map/all_to_all | solution.py:42
  281.1 3.7 multiply_convert_fusion.10
  284.8 62.0 %all-gather.27.cloned.1.call-done = bf16[1024,2048]{0,1:T(8,128)(2,1)} async-done(((bf16[256,2048]{0,1:T(8,128)(2,1)}), bf16[1024,2048]{0,1:T(8,128)(2,1)}) %all-gather.27.cloned.1.call-update) | async-done | bytes 4194320 | tf_op jit(solution)/shard_map/all_gather | solution.py:50
  346.8 55.2 %all-gather.29.cloned.1.call-done = bf16[2048,2048]{1,0:T(8,128)(2,1)} async-done(((bf16[256,2048]{1,0:T(8,128)(2,1)}), bf16[2048,2048]{1,0:T(8,128)(2,1)}) %all-gather.29.cloned.1.call-update) | async-done | bytes 8388624 | tf_op jit(solution)/shard_map/all_gather | solution.py:50
  402.0 14.4 %fusion.125 = f32[2048,1024]{1,0:T(8,128)} fusion(bf16[2048,2048]{1,0:T(8,128)(2,1)} %all-gather.29.cloned.1.call-done, bf16[1024,2048]{0,1:T(8,128)(2,1)} %all-gather.27.cloned.1.call-done), kind=kOutput, calls=%fused_computation.305 | convolution fusion | flops 8589934592 | bytes 20971520 | tf_op jit(solution)/shard_map/dot_general | solution.py:19
  416.4 67.8 %all-gather.25.cloned.1.call-done = bf16[1024,2048]{0,1:T(8,128)(2,1)} async-done(((bf16[256,2048]{0,1:T(8,128)(2,1)}), bf16[1024,2048]{0,1:T(8,128)(2,1)}) %all-gather.25.cloned.1.call-update) | async-done | bytes 4194320 | tf_op jit(solution)/shard_map/all_gather | solution.py:50
  484.2 55.1 %all-gather.23.cloned.1.call-done = bf16[2048,2048]{1,0:T(8,128)(2,1)} async-done(((bf16[256,2048]{1,0:T(8,128)(2,1)}), bf16[2048,2048]{1,0:T(8,128)(2,1)}) %all-gather.23.cloned.1.call-update) | async-done | bytes 8388624 | tf_op jit(solution)/shard_map/all_gather | solution.py:50
  539.3 22.2 %fusion.6 = (bf16[2048,1024]{1,0:T(8,128)(2,1)S(1)}, f32[2048,1024]{1,0:T(8,128)}) fusion(f32[2048,1024]{1,0:T(8,128)} %fusion.125, bf16[2048,2048]{1,0:T(8,128)(2,1)} %all-gather.23.cloned.1.call-done, bf16[1024,2048]{0,1:T(8,128)(2,1)} %all-gather.25.cloned.1.call-done), kind=kOutput, calls=%fused_computation.11 | convolution fusion | flops 8631877632 | bytes 33554432 | tf_op jit(solution)/shard_map/dot_general | solution.py:19
  563.4 11.0 convolution_convert_fusion
  574.5 15.4 %convolution_convert_fusion.1 = bf16[2048,2048]{1,0:T(8,128)(2,1)} fusion(bf16[1024,2048]{0,1:T(8,128)(2,1)} %all-gather.27.cloned.1.call-done, f32[2048,1024]{1,0:T(8,128)} %get-tuple-element.93), kind=kOutput, calls=%fused_computation.20 | convolution fusion | flops 8613003264 | bytes 20971520 | tf_op jit(solution)/shard_map/dot_general | solution.py:19
  589.9 56.0 %reduce-scatter.15.cloned.1.call-done = bf16[256,2048]{1,0:T(8,128)(2,1)} async-done(((bf16[2048,2048]{1,0:T(8,128)(2,1)}), bf16[256,2048]{1,0:T(8,128)(2,1)}) %reduce-scatter.15.cloned.1.call-update) | async-done | bytes 1048592 | tf_op jit(solution)/shard_map/reduce_scatter | solution.py:54
  648.7 71.8 %reduce-scatter.13.cloned.1.call-done = bf16[256,2048]{1,0:T(8,128)(2,1)} async-done(((bf16[2048,2048]{1,0:T(8,128)(2,1)}), bf16[256,2048]{1,0:T(8,128)(2,1)}) %reduce-scatter.13.cloned.1.call-update) | async-done | bytes 1048592 | tf_op jit(solution)/shard_map/reduce_scatter | solution.py:54
  720.5 5.3 fusion.111
  725.9 16.1 %convolution_convert_fusion.2 = bf16[1024,2048]{1,0:T(8,128)(2,1)} fusion(bf16[2048,2048]{1,0:T(8,128)(2,1)} %all-gather.29.cloned.1.call-done, f32[2048,1024]{1,0:T(8,128)} %get-tuple-element.93), kind=kOutput, calls=%fused_computation.73 | convolution fusion | flops 8610906112 | bytes 20971520 | tf_op jit(solution)/shard_map/dot_general | solution.py:19
  742.3 18.1 %all-gather.31.cloned.1.call-done = bf16[1024,2048]{1,0:T(8,128)(2,1)} async-done(((bf16[256,2048]{1,0:T(8,128)(2,1)}), bf16[1024,2048]{1,0:T(8,128)(2,1)}) %all-gather.31.cloned.1.call-update) | async-done | bytes 4194320 | tf_op jit(solution)/shard_map/all_gather | solution.py:50
  760.4 5.3 convolution_convert_fusion.9
  765.8 3.1 multiply_reduce_fusion
  781.5 3.7 multiply_reduce_fusion.7
  785.3 4.5 multiply_convert_fusion.1
  789.7 4.5 multiply_convert_fusion.2
  806.4 3.8 multiply_reduce_fusion.6
  816.7 4.0 multiply_reduce_fusion.5
  820.8 4.5 multiply_convert_fusion.6
  825.3 3.8 convolution_add_fusion.11
  829.1 4.0 multiply_reduce_fusion.4
  833.1 4.5 multiply_convert_fusion.5
  850.9 14.1 convolution_convert_fusion.3
  877.6 6.1 convolution_convert_fusion.7
  885.4 18.9 %all_to_all.126 = bf16[4,256,512]{2,1,0:T(8,128)(2,1)} all-to-all(bf16[4,256,512]{2,1,0:T(8,128)(2,1)S(1)} %pad_maximum_fusion.5), channel_id=1, replica_groups=mesh['dp'=2,'row'=4,'col'=4] {'col'}, dimensions={0} | all-to-all | bytes 2097152 | tf_op jit(solution)/shard_map/all_to_all | solution.py:14
  904.4 5.9 convolution_convert_fusion.6
  915.7 6.0 convolution_convert_fusion.4
  921.8 69.2 %reduce-scatter.27.cloned.1.call-done = bf16[256,2048]{1,0:T(8,128)(2,1)} async-done(((bf16[1024,2048]{1,0:T(8,128)(2,1)}), bf16[256,2048]{1,0:T(8,128)(2,1)}) %reduce-scatter.27.cloned.1.call-update) | async-done | bytes 1048592 | tf_op jit(solution)/shard_map/reduce_scatter | solution.py:54
  992.4 17.1 %all_to_all.127 = bf16[4,256,512]{2,1,0:T(8,128)(2,1)S(1)} all-to-all(bf16[4,256,512]{2,1,0:T(8,128)(2,1)S(1)} %pad_maximum_fusion.4), channel_id=1, replica_groups=mesh['dp'=2,'row'=4,'col'=4] {'col'}, dimensions={0} | all-to-all | bytes 2097152 | tf_op jit(solution)/shard_map/all_to_all | solution.py:14
  1010.9 26.7 %reduce-scatter.21.cloned.1.call-done = bf16[128,2048]{1,0:T(8,128)(2,1)} async-done(((bf16[512,2048]{1,0:T(8,128)(2,1)}), bf16[128,2048]{1,0:T(8,128)(2,1)}) %reduce-scatter.21.cloned.1.call-update) | async-done | bytes 524304 | tf_op jit(solution)/shard_map/reduce_scatter | solution.py:54
  1039.5 3.5 all-to-all-start.7
  1044.5 26.9 %all-gather.35.cloned.1.call-done = bf16[2048,512]{1,0:T(8,128)(2,1)} async-done(((bf16[1024,512]{1,0:T(8,128)(2,1)}), bf16[2048,512]{1,0:T(8,128)(2,1)}) %all-gather.35.cloned.1.call-update) | async-done | bytes 2097168 | tf_op jit(solution)/shard_map/all_gather | solution.py:50
  1071.5 4.2 convert_element_type.337
  1075.7 42.1 %reduce-scatter.25.cloned.1.call-done = bf16[128,2048]{1,0:T(8,128)(2,1)} async-done(((bf16[512,2048]{1,0:T(8,128)(2,1)}), bf16[128,2048]{1,0:T(8,128)(2,1)}) %reduce-scatter.25.cloned.1.call-update) | async-done | bytes 524304 | tf_op jit(solution)/shard_map/reduce_scatter | solution.py:54
  1119.8 25.2 %reduce-scatter.23.cloned.1.call-done = bf16[512,256]{1,0:T(8,128)(2,1)} async-done(((bf16[2048,256]{1,0:T(8,128)(2,1)}), bf16[512,256]{1,0:T(8,128)(2,1)}) %reduce-scatter.23.cloned.1.call-update) | async-done | bytes 262160 | tf_op jit(solution)/shard_map/reduce_scatter | solution.py:54
  1145.0 3.5 all-to-all-start.8
  1150.8 6.6 all-to-all-done.8
  1157.3 3.5 all-to-all-start.4
  1161.4 37.7 %reduce-scatter.17.cloned.1.call-done = bf16[256,2048]{1,0:T(8,128)(2,1)} async-done(((bf16[1024,2048]{1,0:T(8,128)(2,1)}), bf16[256,2048]{1,0:T(8,128)(2,1)}) %reduce-scatter.17.cloned.1.call-update) | async-done | bytes 1048592 | tf_op jit(solution)/shard_map/reduce_scatter | solution.py:54
  1205.5 4.3 all-to-all-start.6
  1209.8 24.6 %all-gather.33.cloned.1.call-done = bf16[2048,512]{0,1:T(8,128)(2,1)} async-done(((bf16[1024,512]{0,1:T(8,128)(2,1)}), bf16[2048,512]{0,1:T(8,128)(2,1)}) %all-gather.33.cloned.1.call-update) | async-done | bytes 2097168 | tf_op jit(solution)/shard_map/all_gather | solution.py:50
  1234.4 4.3 convert_bitcast_fusion
  1238.7 69.7 %all-reduce.4.cloned.1.call-done = bf16[512,256]{1,0:T(8,128)(2,1)} async-done(((bf16[512,256]{1,0:T(8,128)(2,1)}), bf16[512,256]{1,0:T(8,128)(2,1)}) %all-reduce.4.cloned.1.call-update) | async-done | bytes 262160 | tf_op jit(solution)/shard_map/psum | solution.py:192
  1310.2 40.7 %all-reduce.6.cloned.1.call-done = (bf16[512,512]{1,0:T(8,128)(2,1)}, bf16[512,512]{1,0:T(8,128)(2,1)}) async-done(((bf16[512,512]{1,0:T(8,128)(2,1)}, bf16[512,512]{1,0:T(8,128)(2,1)}), (bf16[512,512]{1,0:T(8,128)(2,1)}, bf16[512,512]{1,0:T(8,128)(2,1)})) %all-reduce.6.cloned.1.call-update) | async-done | bytes 1048592 | tf_op jit(solution)/shard_map/psum | solution.py:195
  1355.2 39.5 %psum.28 = f32[4,2048]{1,0:T(4,128)S(1)} all-reduce(f32[4,2048]{1,0:T(4,128)S(1)} %pad_maximum_fusion.8), channel_id=1, replica_groups=mesh['dp'=2,'row'=4,'col'=4] {'dp','row','col'}, use_global_device_ids=true, to_apply=%region_41.42 | all-reduce | flops 8192 | bytes 65536 | tf_op jit(solution)/shard_map/psum | solution.py:193
  (312 shorter events, 143.3 us)
Async XLA Ops:
  7.2 202.7 %copy-start = (bf16[2048,512]{1,0:T(8,128)(2,1)S(1)}, bf16[2048,512]{1,0:T(8,128)(2,1)}, u32[]{:S(2)}) copy-start(bf16[2048,512]{1,0:T(8,128)(2,1)} %param.23) | copy-start | bytes 6291460
  7.2 16.9 %copy-start.54 = (s32[2]{0:T(128)S(1)}, s32[2]{0:T(128)}, u32[]{:S(2)}) copy-start(s32[2]{0:T(128)} %param.13) | copy-start | bytes 28
  7.2 17.0 %copy-start.55 = (f32[512]{0:T(512)S(1)}, f32[512]{0:T(512)}, u32[]{:S(2)}) copy-start(f32[512]{0:T(512)} %param.21) | copy-start | bytes 6148
  7.2 17.0 %copy-start.56 = (f32[512]{0:T(512)S(1)}, f32[512]{0:T(512)}, u32[]{:S(2)}) copy-start(f32[512]{0:T(512)} %param.20) | copy-start | bytes 6148
  7.2 17.0 %copy-start.57 = (f32[512]{0:T(512)S(1)}, f32[512]{0:T(512)}, u32[]{:S(2)}) copy-start(f32[512]{0:T(512)} %param.16) | copy-start | bytes 6148
  7.2 17.0 %copy-start.58 = (f32[512]{0:T(512)S(1)}, f32[512]{0:T(512)}, u32[]{:S(2)}) copy-start(f32[512]{0:T(512)} %param.15) | copy-start | bytes 6148
  7.2 39.9 %all-gather.13.cloned.1.call-start = ((), (), s32[]{:S(2)}) async-start(), calls=%async_computation.21 | async-start | bytes 5242880 | tf_op jit(solution)/shard_map/all_gather | solution.py:50
  8.0 57.8 %all-gather.17.cloned.1.call-start = ((), (), s32[]{:S(2)}) async-start(), calls=%async_computation.23 | async-start | bytes 1310720 | tf_op jit(solution)/shard_map/all_gather | solution.py:50
  8.7 105.5 %all-gather.15.cloned.1.call-start = ((), (), s32[]{:S(2)}) async-start(), calls=%async_computation.22 | async-start | bytes 2621440 | tf_op jit(solution)/shard_map/all_gather | solution.py:50
  24.0 132.4 %all-gather.19.cloned.1.call-start = ((), (), s32[]{:S(2)}) async-start(), calls=%async_computation.24 | async-start | bytes 2228224 | tf_op jit(solution)/shard_map/all_gather | solution.py:50
  29.6 28.7 %copy-start.50 = (f32[1,2048]{1,0:T(1,128)}, f32[1,2048]{1,0:T(1,128)S(1)}, u32[]{:S(2)}) copy-start(f32[1,2048]{1,0:T(1,128)S(1)} %get-tuple-element.56) | copy-start | bytes 24580
  50.8 7.5 copy-start.52
  50.8 7.5 copy-start.53
  68.4 12.3 all-to-all-start.1
  71.9 131.5 %all-gather.21.cloned.1.call-start = ((), (), s32[]{:S(2)}) async-start(), calls=%async_computation.25 | async-start | bytes 2621440 | tf_op jit(solution)/shard_map/all_gather | solution.py:50
  81.8 197.1 %reduce-scatter.11.cloned.1.call-start = ((), (), s32[]{:S(2)}) async-start(), calls=%async_computation.26 | async-start | bytes 5242880 | tf_op jit(solution)/shard_map/reduce_scatter | solution.py:54
  119.4 48.5 %copy-start.48 = (bf16[1024,512]{1,0:T(8,128)(2,1)}, bf16[1024,512]{1,0:T(8,128)(2,1)S(1)}, u32[]{:S(2)}) copy-start(bf16[1024,512]{1,0:T(8,128)(2,1)S(1)} %convolution_convert_fusion.10) | copy-start | bytes 3145732
  158.2 23.6 %copy-start.19 = (bf16[4,2,512,256]{3,2,0,1:T(8,128)(2,1)}, bf16[4,2,512,256]{3,2,0,1:T(8,128)(2,1)S(1)}, u32[]{:S(2)}) copy-start(bf16[4,2,512,256]{3,2,0,1:T(8,128)(2,1)S(1)} %copy.56) | copy-start | bytes 6291460
  159.6 15.7 %copy-start.2 = (f32[512,2048]{1,0:T(8,128)}, f32[512,2048]{1,0:T(8,128)S(1)}, u32[]{:S(2)}) copy-start(f32[512,2048]{1,0:T(8,128)S(1)} %get-tuple-element.77) | copy-start | bytes 12582916
  161.0 15.2 %copy-start.6 = (f32[512,2048]{1,0:T(8,128)}, f32[512,2048]{1,0:T(8,128)S(1)}, u32[]{:S(2)}) copy-start(f32[512,2048]{1,0:T(8,128)S(1)} %get-tuple-element.79) | copy-start | bytes 12582916
  162.4 14.8 %copy-start.10 = (f32[512,2048]{1,0:T(8,128)}, f32[512,2048]{1,0:T(8,128)S(1)}, u32[]{:S(2)}) copy-start(f32[512,2048]{1,0:T(8,128)S(1)} %get-tuple-element.81) | copy-start | bytes 12582916
  163.8 14.3 %copy-start.14 = (f32[512,2048]{1,0:T(8,128)}, f32[512,2048]{1,0:T(8,128)S(1)}, u32[]{:S(2)}) copy-start(f32[512,2048]{1,0:T(8,128)S(1)} %get-tuple-element.83) | copy-start | bytes 12582916
  165.2 13.8 copy-start.4
  166.6 13.4 copy-start.8
  167.9 12.9 copy-start.12
  169.5 12.3 copy-start.16
  209.8 19.0 %copy-start.46 = (bf16[2,512,512]{2,1,0:T(8,128)(2,1)S(1)}, bf16[2,512,512]{2,1,0:T(8,128)(2,1)}, u32[]{:S(2)}) copy-start(bf16[2,512,512]{2,1,0:T(8,128)(2,1)} %param.14) | copy-start | bytes 3145732
  209.8 136.9 %all-gather.27.cloned.1.call-start = ((), (), s32[]{:S(2)}) async-start(), calls=%async_computation.29 | async-start | bytes 5242880 | tf_op jit(solution)/shard_map/all_gather | solution.py:50
  228.5 173.5 %all-gather.29.cloned.1.call-start = ((), (), s32[]{:S(2)}) async-start(), calls=%async_computation.31 | async-start | bytes 9437184 | tf_op jit(solution)/shard_map/all_gather | solution.py:50
  258.7 225.6 %all-gather.25.cloned.1.call-start = ((), (), s32[]{:S(2)}) async-start(), calls=%async_computation.28 | async-start | bytes 5242880 | tf_op jit(solution)/shard_map/all_gather | solution.py:50
  278.8 260.5 %all-gather.23.cloned.1.call-start = ((), (), s32[]{:S(2)}) async-start(), calls=%async_computation.27 | async-start | bytes 9437184 | tf_op jit(solution)/shard_map/all_gather | solution.py:50
  284.7 361.2 %reduce-scatter.15.cloned.1.call-start = ((), (), s32[]{:S(2)}) async-start(), calls=%async_computation.32 | async-start | bytes 9437184 | tf_op jit(solution)/shard_map/reduce_scatter | solution.py:54
  539.3 24.1 %copy-start.59 = (bf16[1024,2048]{0,1:T(8,128)(2,1)S(1)}, bf16[1024,2048]{0,1:T(8,128)(2,1)}, u32[]{:S(2)}) copy-start(bf16[1024,2048]{0,1:T(8,128)(2,1)} %all-gather.25.cloned.1.call-done) | copy-start | bytes 12582916
  574.4 146.1 %reduce-scatter.13.cloned.1.call-start = ((), (), s32[]{:S(2)}) async-start(), calls=%async_computation.30 | async-start | bytes 9437184 | tf_op jit(solution)/shard_map/reduce_scatter | solution.py:54
  589.9 56.0 %copy-start.37 = (bf16[256,2048]{1,0:T(8,128)(2,1)S(1)}, bf16[256,2048]{1,0:T(8,128)(2,1)}, u32[]{:S(2)}) copy-start(bf16[256,2048]{1,0:T(8,128)(2,1)} %reduce-scatter.11.cloned.1.call-done) | copy-start | bytes 3145732
  589.9 130.6 %copy-start.38 = (bf16[4,32,8,512]{3,2,0,1:T(8,128)(2,1)S(1)}, bf16[4,32,8,512]{3,2,0,1:T(8,128)(2,1)}, u32[]{:S(2)}) copy-start(bf16[4,32,8,512]{3,2,0,1:T(8,128)(2,1)} %copy.71) | copy-start | bytes 3145732
  589.9 170.5 %all-gather.31.cloned.1.call-start = ((), (), s32[]{:S(2)}) async-start(), calls=%async_computation.33 | async-start | bytes 5242880 | tf_op jit(solution)/shard_map/all_gather | solution.py:50
  725.8 158.1 %reduce-scatter.29.cloned.1.call-start = ((), (), s32[]{:S(2)}) async-start(), calls=%async_computation.42 | async-start | bytes 5242880 | tf_op jit(solution)/shard_map/reduce_scatter | solution.py:54
  742.0 23.7 %copy-start.20 = (bf16[4,2,512,256]{3,2,0,1:T(8,128)(2,1)S(1)}, bf16[4,2,512,256]{3,2,0,1:T(8,128)(2,1)}, u32[]{:S(2)}) copy-start(bf16[4,2,512,256]{3,2,0,1:T(8,128)(2,1)} %copy-done.19) | copy-start | bytes 6291460
  742.0 170.9 %reduce-scatter.19.cloned.1.call-start = ((), (), s32[]{:S(2)}) async-start(), calls=%async_computation.35 | async-start | bytes 2228224 | tf_op jit(solution)/shard_map/reduce_scatter | solution.py:54
  765.7 9.6 copy-start.40
  778.5 6.8 copy-start.24
  813.3 7.4 copy-start.32
  820.8 8.3 copy-start.41
  850.8 140.2 %reduce-scatter.27.cloned.1.call-start = ((), (), s32[]{:S(2)}) async-start(), calls=%async_computation.40 | async-start | bytes 5242880 | tf_op jit(solution)/shard_map/reduce_scatter | solution.py:54
  864.9 172.6 %reduce-scatter.21.cloned.1.call-start = ((), (), s32[]{:S(2)}) async-start(), calls=%async_computation.36 | async-start | bytes 2621440 | tf_op jit(solution)/shard_map/reduce_scatter | solution.py:54
  866.6 6.1 copy-start.25
  883.8 20.6 %copy-start.47 = (bf16[2,512,512]{2,1,0:T(8,128)(2,1)S(1)}, bf16[2,512,512]{2,1,0:T(8,128)(2,1)}, u32[]{:S(2)}) copy-start(bf16[2,512,512]{2,1,0:T(8,128)(2,1)} %copy.57) | copy-start | bytes 3145732
  883.8 187.6 %all-gather.35.cloned.1.call-start = ((), (), s32[]{:S(2)}) async-start(), calls=%async_computation.43 | async-start | bytes 3145728 | tf_op jit(solution)/shard_map/all_gather | solution.py:50
  904.3 213.4 %reduce-scatter.25.cloned.1.call-start = ((), (), s32[]{:S(2)}) async-start(), calls=%async_computation.39 | async-start | bytes 2621440 | tf_op jit(solution)/shard_map/reduce_scatter | solution.py:54
  910.3 234.7 %reduce-scatter.23.cloned.1.call-start = ((), (), s32[]{:S(2)}) async-start(), calls=%async_computation.37 | async-start | bytes 1310720 | tf_op jit(solution)/shard_map/reduce_scatter | solution.py:54
  915.7 283.5 %reduce-scatter.17.cloned.1.call-start = ((), (), s32[]{:S(2)}) async-start(), calls=%async_computation.34 | async-start | bytes 5242880 | tf_op jit(solution)/shard_map/reduce_scatter | solution.py:54
  921.7 312.7 %all-gather.33.cloned.1.call-start = ((), (), s32[]{:S(2)}) async-start(), calls=%async_computation.41 | async-start | bytes 3145728 | tf_op jit(solution)/shard_map/all_gather | solution.py:50
  1039.5 105.5 %all-to-all-start.7 = ((bf16[4,128,512]{2,1,0:T(8,128)(2,1)}), bf16[4,128,512]{2,1,0:T(8,128)(2,1)S(1)}, u32[]{:S(2)}, u32[]{:S(2)}) async-start(bf16[4,128,512]{2,1,0:T(8,128)(2,1)} %pad_maximum_fusion.6), calls=%async_computation.13 | async-start | bytes 1048576 | tf_op jit(solution)/shard_map/all_to_all | solution.py:14
  1043.0 265.4 %all-reduce.4.cloned.1.call-start = ((), (), s32[]{:S(2)}) async-start(), calls=%async_computation.38 | async-start | bytes 524288 | tf_op jit(solution)/shard_map/psum | solution.py:192
  1044.5 104.0 %copy-start.43 = (bf16[256,2048]{1,0:T(8,128)(2,1)S(1)}, bf16[256,2048]{1,0:T(8,128)(2,1)}, u32[]{:S(2)}) copy-start(bf16[256,2048]{1,0:T(8,128)(2,1)} %get-tuple-element.27) | copy-start | bytes 3145732
  1145.0 12.3 all-to-all-start.8
  1148.5 50.6 %copy-start.49 = (bf16[256,256]{1,0:T(8,128)(2,1)S(1)}, bf16[256,256]{1,0:T(8,128)(2,1)}, u32[]{:S(2)}) copy-start(bf16[256,256]{1,0:T(8,128)(2,1)} %reduce-scatter.19.cloned.1.call-done) | copy-start | bytes 393220
  1148.5 50.6 %copy-start.51 = (f32[1,2048]{1,0:T(1,128)S(1)}, f32[1,2048]{1,0:T(1,128)}, u32[]{:S(2)}) copy-start(f32[1,2048]{1,0:T(1,128)} %copy-done.50) | copy-start | bytes 24580
  1157.3 48.2 %all-to-all-start.4 = ((bf16[4,256,512]{2,1,0:T(8,128)(2,1)}), bf16[4,256,512]{2,1,0:T(8,128)(2,1)S(1)}, u32[]{:S(2)}, u32[]{:S(2)}) async-start(bf16[4,256,512]{2,1,0:T(8,128)(2,1)} %pad_maximum_fusion.1), calls=%async_computation.6 | async-start | bytes 2097152 | tf_op jit(solution)/shard_map/all_to_all | solution.py:14
  1160.9 190.0 %all-reduce.6.cloned.1.call-start = ((), (), s32[]{:S(2)}) async-start(), calls=%async_computation.44 | async-start | bytes 2097152 | tf_op jit(solution)/shard_map/psum | solution.py:195
  1160.9 41.3 %copy-start.39 = (f32[256,2048]{1,0:T(8,128)S(1)}, f32[256,2048]{1,0:T(8,128)}, u32[]{:S(2)}) copy-start(f32[256,2048]{1,0:T(8,128)} %get-tuple-element.26) | copy-start | bytes 6291460
  1205.5 189.8 %all-to-all-start.6 = ((bf16[4,256,512]{2,1,0:T(8,128)(2,1)}), bf16[4,256,512]{2,1,0:T(8,128)(2,1)}, u32[]{:S(2)}, u32[]{:S(2)}) async-start(bf16[4,256,512]{2,1,0:T(8,128)(2,1)} %pad_maximum_fusion.3), calls=%async_computation.11 | async-start | bytes 2097152 | tf_op jit(solution)/shard_map/all_to_all | solution.py:14
  1234.4 164.2 %copy-start.1 = (bf16[2048,512]{1,0:T(8,128)(2,1)S(1)}, bf16[2048,512]{1,0:T(8,128)(2,1)}, u32[]{:S(2)}) copy-start(bf16[2048,512]{1,0:T(8,128)(2,1)} %param.23) | copy-start | bytes 6291460
  (26 other events, 87.3 us)
Sparse Core Ops, SparseCore 0:
  9.6 37.4 all-gather.12
  48.7 17.0 all-gather.16
  67.9 46.2 all-gather.14
  116.8 39.6 all-gather.18
  158.4 44.9 all-gather.20
  209.9 53.9 reduce-scatter.10
  266.2 80.5 all-gather.26
  349.4 52.5 all-gather.28
  403.6 80.5 all-gather.24
  486.7 52.5 all-gather.22
  574.6 71.3 reduce-scatter.14
  649.2 71.2 reduce-scatter.12
  725.9 34.4 all-gather.30
  762.7 76.7 reduce-scatter.28
  850.9 61.9 reduce-scatter.18
  915.2 75.7 reduce-scatter.26
  993.1 44.3 reduce-scatter.20
  1039.0 32.4 all-gather.34
  1073.9 43.8 reduce-scatter.24
  1120.7 24.2 reduce-scatter.22
  1148.3 50.8 reduce-scatter.16
  1201.3 33.0 all-gather.32
  1237.8 70.5 all-reduce.3
  1311.3 39.5 all-reduce.5
